TPU v7x, 256 devices: a whole 4x4x8 slice. The times are simulated.
256 devices in a mesh: pipe: 4 (over y_lo, core), ctx: 16 (over z, y_hi), tp: 4 (over x).
Axes of the slice: x: 4, y: 4 (y_hi: 2, y_lo: 2; y = y_hi * 2 + y_lo), z: 8, core: 2. Of those that a mesh axis runs over, the one named last changes fastest.
Arguments:
- segment_inputs: bfloat16 [4, 2, 2048, 4096], P('pipe', None, ('ctx', 'tp')), may hold values from -128 to 128
- keys: bfloat16 [4, 2, 2048, 512], P('pipe', None, 'ctx', 'tp'), may hold values from -64 to 64
- values: bfloat16 [4, 2, 2048, 512], P('pipe', None, 'ctx', 'tp'), may hold values from -6 to 6
- norm_gain: float32 [4, 4096], P('pipe'), may hold values from 0.1 to 1.9
- waiting_grads: bfloat16 [4, 2048, 4096], P('pipe', ('ctx', 'tp')), may hold values from -32 to 32
- output_grads: bfloat16 [1, 2048, 4096], P(None, ('ctx', 'tp')), may hold values from -32 to 32
- doc_lengths: int32 [5, 8], replicated, may hold values from 1 to 1024, as said below
Outputs:
- input_grads: bfloat16 [4, 2, 2048, 4096], P('pipe', None, ('ctx', 'tp'))
- key_grads: float32 [4, 2, 2048, 512], P('pipe', None, 'ctx', 'tp')
- value_grads: float32 [4, 2, 2048, 512], P('pipe', None, 'ctx', 'tp')
- gain_grads: float32 [4, 4096], P('pipe')
Inputs may be any that keep to these rules, and one draw needn't show every extreme that they name: `doc_lengths`: row m lists in order of position the lengths of the 8 documents packed into microbatch m's sequence; each row sums to 2048; the last document is exactly 1024 long.
All inputs are finite; a program needn't handle non-finite values.
Results may differ from a plain program's by a relative error of at most 0.009.
The roundings to bfloat16 on the way count: a program that leaves them out, or rounds other values in their place, can miss the bound.
Values may be sent and summed in bfloat16 or wider, within the bound.
A program may use at most 64 MiB of HBM per device.

v0:
```python
import jax
import jax.numpy as jnp
from jax import lax
from jax.sharding import PartitionSpec as P

HD = 128
S_DEV = 128
TICKS = 2
epsilon = 1e-05
masked_fill = -1e30


def passed_along(value, axis, by):
    count = lax.axis_size(axis)
    return lax.ppermute(value, axis, [(i, (i + by) % count) for i in range(count)])


def from_behind(value, axis, steps):
    count = lax.axis_size(axis)
    first, last = (max(0, -steps), min(count, count - steps))
    return lax.ppermute(value, axis, [(source, source + steps) for source in range(first, last)])


def row_positions(rows, half_rows, cycle_count):
    section = rows // half_rows
    offset = rows % half_rows
    owner = section // 2
    placed = jnp.where(section % 2 == 0, owner, 2 * cycle_count - 1 - owner)
    return placed * half_rows + offset


def document_starts(lengths_row, positions):
    closing = jnp.cumsum(lengths_row)
    passed = closing[None, :] <= positions[:, None]
    return jnp.sum(jnp.where(passed, lengths_row[None, :], 0), axis=1)


def keep_same(current):
    return current


def key_positions(key_first, key_count, cycle_count):
    rows = key_first + jnp.arange(key_count, dtype=jnp.int32)
    return row_positions(rows, S_DEV // 2, cycle_count)


def block_active(key_first, key_count, query_pos, query_start, cycle_count):
    key_pos = key_positions(key_first, key_count, cycle_count)
    return (jnp.min(key_pos) <= jnp.max(query_pos)) & (jnp.max(key_pos) >= jnp.min(query_start))


def score_block(query_block, key_block, query_pos, query_start, key_first, cycle_count):
    key_count = key_block.shape[0]
    key_pos = key_positions(key_first, key_count, cycle_count)
    scores = HD ** (-0.5) * jnp.einsum(
        "rkgd,skd->kgrs", query_block, key_block, preferred_element_type=jnp.float32
    )
    visible = (key_pos[None, :] <= query_pos[:, None]) & (key_pos[None, :] >= query_start[:, None])
    return (scores, visible[None, None])


def forward_update(carry, key_flat, value_flat, key_first, context):
    query_block, grad_block, query_pos, query_start, cycle_count = context
    key_count = key_flat.shape[0]

    def apply_block(current):
        row_peak, row_total, weighted = current
        key_block = key_flat.reshape(key_count, -1, HD)
        value_block = value_flat.reshape(key_count, -1, HD)
        scores, visible = score_block(
            query_block, key_block, query_pos, query_start, key_first, cycle_count
        )
        block_peak = jnp.max(jnp.where(visible, scores, masked_fill), axis=-1)
        new_peak = jnp.maximum(row_peak, block_peak)
        weights = jnp.where(visible, jnp.exp(scores - new_peak[..., None]), 0.0)
        prob_grad = jnp.einsum(
            "rkgd,skd->kgrs", grad_block, value_block, preferred_element_type=jnp.float32
        )
        return (new_peak, jnp.sum(weights, axis=-1), jnp.sum(weights * prob_grad, axis=-1))

    return lax.cond(
        block_active(key_first, key_count, query_pos, query_start, cycle_count),
        apply_block,
        keep_same,
        carry,
    )


def backward_terms(key_flat, value_flat, key_first, context, row_stats):
    query_block, grad_block, query_pos, query_start, cycle_count = context
    logsum, row_term = row_stats
    key_count = key_flat.shape[0]
    key_block = key_flat.reshape(key_count, -1, HD)
    value_block = value_flat.reshape(key_count, -1, HD)
    scale_factor = HD ** (-0.5)
    scores, visible = score_block(
        query_block, key_block, query_pos, query_start, key_first, cycle_count
    )
    prob_weights = jnp.where(visible, jnp.exp(scores - logsum[..., None]), 0.0)
    prob_grad = jnp.einsum(
        "rkgd,skd->kgrs", grad_block, value_block, preferred_element_type=jnp.float32
    )
    dscore = (prob_weights * (prob_grad - row_term[..., None])).astype(jnp.bfloat16)
    probs_low = prob_weights.astype(jnp.bfloat16)
    query_add = scale_factor * jnp.einsum(
        "kgrs,skd->rkgd", dscore, key_block, preferred_element_type=jnp.float32
    )
    key_add = scale_factor * jnp.einsum(
        "kgrs,rkgd->skd", dscore, query_block, preferred_element_type=jnp.float32
    )
    value_add = jnp.einsum(
        "kgrs,rkgd->skd", probs_low, grad_block, preferred_element_type=jnp.float32
    )
    return (query_add, key_add.reshape(key_count, -1), value_add.reshape(key_count, -1))


def segment_tick(inputs, key_local, value_local, gain_row, arriving, lengths_row):
    widened = inputs.astype(jnp.float32)
    inverse = lax.rsqrt(jnp.mean(widened * widened, axis=-1, keepdims=True) + epsilon)
    normed = widened * inverse
    queries = (normed * gain_row[None, :]).astype(jnp.bfloat16)
    query_heads, grad_heads = (
        lax.all_to_all(queries, "tp", split_axis=1, concat_axis=0, tiled=True),
        lax.all_to_all(arriving, "tp", split_axis=1, concat_axis=0, tiled=True),
    )
    row_count = key_local.shape[0]
    kv_local = key_local.shape[1] // HD
    group_size = query_heads.shape[1] // (HD * kv_local)
    query_block = query_heads.reshape(row_count, kv_local, group_size, HD)
    grad_block = grad_heads.reshape(row_count, kv_local, group_size, HD)
    cycle_count = lax.axis_size("ctx")
    cycle_place = lax.axis_index("ctx")
    query_pos = key_positions(cycle_place * row_count, row_count, cycle_count)
    query_start = document_starts(lengths_row, query_pos)
    context = (query_block, grad_block, query_pos, query_start, cycle_count)
    empty_peak = jnp.full((kv_local, group_size, row_count), masked_fill, jnp.float32)
    zero_rows = jnp.zeros((kv_local, group_size, row_count), jnp.float32)
    initial = (empty_peak, zero_rows, zero_rows)
    row_peak, row_total, weighted = forward_update(
        initial,
        lax.all_gather(key_local, "ctx", axis=0, tiled=True),
        lax.all_gather(value_local, "ctx", axis=0, tiled=True),
        jnp.int32(0),
        context,
    )
    row_stats = (row_peak + jnp.log(row_total), weighted / row_total)
    query_zero = jnp.zeros((row_count, kv_local, group_size, HD), jnp.float32)

    def cycle_turn(cycle_step, carry):
        key_block, value_block, key_grad, value_grad, query_grad = carry
        owner_index = (cycle_place - cycle_step) % cycle_count
        block_first = owner_index * row_count

        def apply_terms(current):
            added_terms = backward_terms(key_block, value_block, block_first, context, row_stats)
            return (
                current[0] + added_terms[1],
                current[1] + added_terms[2],
                current[2] + added_terms[0],
            )

        key_grad, value_grad, query_grad = lax.cond(
            block_active(block_first, row_count, query_pos, query_start, cycle_count),
            apply_terms,
            keep_same,
            (key_grad, value_grad, query_grad),
        )
        key_block, value_block = passed_along((key_block, value_block), "ctx", 1)
        key_grad, value_grad = passed_along((key_grad, value_grad), "ctx", 1)
        return (key_block, value_block, key_grad, value_grad, query_grad)

    zero_kv = jnp.zeros(key_local.shape, jnp.float32)
    finished = lax.fori_loop(
        0, cycle_count, cycle_turn, (key_local, value_local, zero_kv, zero_kv, query_zero)
    )
    key_grad, value_grad, query_grad = (finished[2], finished[3], finished[4])
    query_low = query_grad.reshape(row_count, -1).astype(jnp.bfloat16)
    grad_rows = lax.all_to_all(query_low, "tp", split_axis=0, concat_axis=1, tiled=True)
    rounded = grad_rows.astype(jnp.float32)
    scaled = rounded * gain_row[None, :]
    coupling = jnp.mean(scaled * normed, axis=-1, keepdims=True)
    input_grad = (arriving.astype(jnp.float32) + inverse * (scaled - normed * coupling)).astype(
        jnp.bfloat16
    )
    gain_part = jnp.sum(rounded * normed, axis=0)
    return (input_grad, key_grad, value_grad, gain_part)


def on_device(segment_inputs, keys, values, norm_gain, waiting_grads, output_grads, doc_lengths):
    segment_index = lax.axis_index("pipe")
    last_segment = lax.axis_size("pipe") - 1
    gain_row = norm_gain[0]
    arriving = waiting_grads[0]
    input_list = []
    key_list = []
    value_list = []
    gain_running = jnp.zeros(gain_row.shape, jnp.float32)
    for tick_index in range(TICKS):
        micro_index = segment_index + tick_index
        lengths_row = lax.dynamic_index_in_dim(doc_lengths, micro_index, 0, keepdims=False)
        input_grad, key_grad, value_grad, gain_part = segment_tick(
            segment_inputs[0, tick_index],
            keys[0, tick_index],
            values[0, tick_index],
            gain_row,
            arriving,
            lengths_row,
        )
        input_list.append(input_grad)
        key_list.append(key_grad)
        value_list.append(value_grad)
        gain_running = gain_running + gain_part
        if tick_index + 1 < TICKS:
            arrived = from_behind(input_grad, "pipe", -1)
            arriving = jnp.where(segment_index == last_segment, output_grads[tick_index], arrived)
    gain_grads = lax.psum(gain_running, ("ctx", "tp"))
    return (
        jnp.stack(input_list)[None],
        jnp.stack(key_list)[None],
        jnp.stack(value_list)[None],
        gain_grads[None],
    )


def solution(mesh):
    in_specs = (
        P("pipe", None, ("ctx", "tp"), None),
        P("pipe", None, "ctx", "tp"),
        P("pipe", None, "ctx", "tp"),
        P("pipe", None),
        P("pipe", ("ctx", "tp"), None),
        P(None, ("ctx", "tp"), None),
        P(),
    )
    out_specs = (
        P("pipe", None, ("ctx", "tp"), None),
        P("pipe", None, "ctx", "tp"),
        P("pipe", None, "ctx", "tp"),
        P("pipe", None),
    )
    return jax.shard_map(
        on_device, mesh=mesh, in_specs=in_specs, out_specs=out_specs, check_vma=False
    )
```

profile of v0, /device:TPU:8, one launch (start us, length us, event | category | flops | bytes accessed | tf_op | source)
XLA Modules:
  0.0 1165.9 jit_solution(12238675916187327474)
XLA Ops:
  21.4 46.2 %all-gather = bf16[1,1,2048,128]{3,2,1,0:T(8,128)(2,1)S(1)} all-gather(bf16[1,1,128,128]{3,2,1,0:T(8,128)(2,1)S(1)} %get-tuple-element.1508), channel_id=2, replica_groups=mesh['pipe'=4,'ctx'=16,'tp'=4] {'ctx'}, dimensions={2}, use_global_device_ids=true | all-gather | bytes 557056 | tf_op jit(solution)/shard_map/all_gather | solution.py:141
  72.2 40.6 %all-gather.1 = bf16[1,1,2048,128]{3,2,1,0:T(8,128)(2,1)} all-gather(bf16[1,1,128,128]{3,2,1,0:T(8,128)(2,1)S(1)} %get-tuple-element.1495), channel_id=3, replica_groups=mesh['pipe'=4,'ctx'=16,'tp'=4] {'ctx'}, dimensions={2}, use_global_device_ids=true | all-gather | bytes 557056 | tf_op jit(solution)/shard_map/all_gather | solution.py:142
  113.0 6.8 conditional.4
  120.0 273.9 %while.50 = (s32[]{:T(128)}, bf16[128,128]{1,0:T(8,128)(2,1)S(1)}, bf16[128,128]{1,0:T(8,128)(2,1)S(1)}, f32[128,128]{1,0:T(8,128)S(1)}, f32[128,128]{1,0:T(8,12...) while((s32[]{:T(128)}, bf16[128,128]{1,0:T(8,128)(2,1)S(1)}, ...), condition=%wide.region_17.18_spmd.clone, body=%wide.region_12.17_spmd.clone.sunk | while | flops 169071120 | bytes 6050608 | solution.py:173
  211.9 4.9 collective-permute-start.3
  219.8 4.8 collective-permute-done
  249.4 4.5 collective-permute-start.1
  282.3 4.7 collective-permute-start.1
  386.3 4.7 collective-permute-start.1
  394.9 5.4 all-to-all-start.2
  400.3 6.7 all-to-all-done.2
  411.5 41.4 %all-gather.2 = bf16[1,1,2048,128]{3,2,1,0:T(8,128)(2,1)S(1)} all-gather(bf16[1,1,128,128]{3,2,1,0:T(8,128)(2,1)S(1)} %get-tuple-element.1505), channel_id=4, replica_groups=mesh['pipe'=4,'ctx'=16,'tp'=4] {'ctx'}, dimensions={2}, use_global_device_ids=true | all-gather | bytes 557056 | tf_op jit(solution)/shard_map/all_gather | solution.py:141
  454.9 41.8 %all-gather.3 = bf16[1,1,2048,128]{3,2,1,0:T(8,128)(2,1)} all-gather(bf16[1,1,128,128]{3,2,1,0:T(8,128)(2,1)S(1)} %get-tuple-element.1492), channel_id=5, replica_groups=mesh['pipe'=4,'ctx'=16,'tp'=4] {'ctx'}, dimensions={2}, use_global_device_ids=true | all-gather | bytes 557056 | tf_op jit(solution)/shard_map/all_gather | solution.py:142
  512.4 5.1 all-to-all-done.4
  518.6 6.9 conditional.5
  525.6 273.6 %while.51 = (s32[]{:T(128)}, bf16[128,128]{1,0:T(8,128)(2,1)S(1)}, bf16[128,128]{1,0:T(8,128)(2,1)S(1)}, f32[128,128]{1,0:T(8,128)S(1)}, f32[128,128]{1,0:T(8,12...) while((s32[]{:T(128)}, bf16[128,128]{1,0:T(8,128)(2,1)S(1)}, ...), condition=%wide.region_33.34_spmd.clone, body=%wide.region_28.33_spmd.clone.sunk | while | flops 169071120 | bytes 6050608 | solution.py:173
  550.4 4.7 collective-permute-start.5
  616.8 4.9 collective-permute-start.7
  624.7 4.5 collective-permute-done.4
  655.0 4.7 collective-permute-start.5
  753.7 4.9 collective-permute-start.7
  791.7 4.7 collective-permute-start.5
  805.0 5.3 all-to-all-done.5
  810.8 353.9 %psum.7 = f32[1,4096]{1,0:T(1,128)} all-reduce(f32[1,4096]{1,0:T(1,128)S(1)} %bitcast.426), channel_id=1, replica_groups=mesh['pipe'=4,'ctx'=16,'tp'=4] {'ctx','tp'}, use_global_device_ids=true, to_apply=%region_37.38 | all-reduce | flops 4096 | bytes 32768 | tf_op jit(solution)/shard_map/psum | solution.py:216
  (996 shorter events, 522.0 us)
Async XLA Ops:
  6.3 61.3 %all-to-all-start = ((bf16[32,4,1024]{2,0,1:T(8,128)(2,1)}), bf16[32,4,1024]{2,0,1:T(8,128)(2,1)S(1)}, u32[]{:S(2)}, u32[]{:S(2)}) async-start(bf16[32,4,1024]{2,0,1:T(8,128)(2,1)} %multiply_convert_fusion.1), calls=%async_computation | async-start | bytes 524288 | tf_op jit(solution)/shard_map/all_to_all | solution.py:123
  67.7 45.2 %all-to-all-start.1 = ((bf16[32,4,1024]{2,0,1:T(8,128)(2,1)}), bf16[32,4,1024]{2,0,1:T(8,128)(2,1)S(1)}, u32[]{:S(2)}, u32[]{:S(2)}) async-start(bf16[32,4,1024]{2,0,1:T(8,128)(2,1)} %copy.84), calls=%async_computation.1 | async-start | bytes 524288 | tf_op jit(solution)/shard_map/all_to_all | solution.py:124
  143.1 9.3 collective-permute-start.3
  157.8 9.0 collective-permute-start.2
  192.7 8.8 collective-permute-start.2
  245.0 9.0 collective-permute-start.2
  245.1 8.9 collective-permute-start.3
  279.8 9.8 collective-permute-start.3
  295.0 10.4 collective-permute-start.2
  346.5 9.0 collective-permute-start.2
  380.8 10.3 collective-permute-start.2
  381.0 10.1 collective-permute-start.3
  394.9 12.0 %all-to-all-start.2 = ((bf16[4,32,1024]{2,1,0:T(8,128)(2,1)}), bf16[4,32,1024]{2,1,0:T(8,128)(2,1)S(1)}, u32[]{:S(2)}, u32[]{:S(2)}) async-start(bf16[4,32,1024]{2,1,0:T(8,128)(2,1)} %convert_element_type.172), calls=%async_computation.2 | async-start | bytes 524288 | tf_op jit(solution)/shard_map/all_to_all | solution.py:178
  409.6 91.3 %collective-permute-start.8 = (bf16[32,4096]{1,0:T(8,128)(2,1)}, bf16[32,4096]{1,0:T(8,128)(2,1)}, u32[]{:S(2)}, u32[]{:S(2)}) collective-permute-start(bf16[32,4096]{1,0:T(8,128)(2,1)} %fusion.122), channel_id=1, source_target_pairs={{64,0},{128,64},{192,128},{65,1},{129,65},{193,129},{66,2},{130,66... | collective-permute-start | bytes 786440 | tf_op jit(solution)/shard_map/ppermute | solution.py:21
  496.7 10.1 all-to-all-start.3
  506.8 10.8 all-to-all-start.4
  562.7 9.6 collective-permute-start.6
  649.9 9.8 collective-permute-start.6
  650.0 9.8 collective-permute-start.7
  685.4 8.9 collective-permute-start.7
  700.6 9.8 collective-permute-start.6
  786.7 9.7 collective-permute-start.6
  786.8 9.6 collective-permute-start.7
  800.3 10.1 all-to-all-start.5
  (122 other events, 3979.3 us)
where the time goes:
time: 1170 us
  blocking collectives  524 us (45%)
  starting transfers between devices  263 us (22%)
  waiting for transfers between devices  180 us (15%)
  loops' own time  85 us (7%)
  other arithmetic  51.5 us (4%)
  matrix products  46.7 us (4%)
    psum x1, blocking collectives, on_device(): gain_grads = lax.psum(gain_running, ('ctx', 'tp'))  354 us
    ppermute x128, starting transfers between devices, passed_along(): lax.ppermute(value, axis, [(i, (i + by) % count) for i in range(count)])  236 us
    ppermute x128, waiting for transfers between devices, passed_along(): lax.ppermute(value, axis, [(i, (i + by) % count) for i in range(count)])  159 us
    all_gather x2, blocking collectives, segment_tick(): lax.all_gather(key_local, 'ctx', axis=0, tiled=True)  87.6 us
    all_gather x2, blocking collectives, segment_tick(): lax.all_gather(value_local, 'ctx', axis=0, tiled=True)  82.4 us
    another operation x2, loops' own time, segment_tick(): lax.fori_loop(0, cycle_count, cycle_turn, (key_local, value_local, zero_k...  82.4 us
    reduce_max x33, other arithmetic, block_active(): jnp.max(key_pos) >= jnp.min(query_start)  23.7 us
  transfers between devices with their start and end apart: 135, of which 110 were waited for; matrix products, arithmetic and copies ran while one was open for 1% of the time, Pallas kernels for 0%

commit v1 on v0

--- a/solution.py
+++ b/solution.py
@@ -213,7 +213,8 @@
         if tick_index + 1 < TICKS:
             arrived = from_behind(input_grad, "pipe", -1)
             arriving = jnp.where(segment_index == last_segment, output_grads[tick_index], arrived)
-    gain_grads = lax.psum(gain_running, ("ctx", "tp"))
+    high = lax.psum(gain_running, "ctx")
+    gain_grads = lax.psum(high, "tp")
     return (
         jnp.stack(input_list)[None],
         jnp.stack(key_list)[None],

time: 1170 us -> 904 us (0.77)
  blocking collectives: 524 us -> 260 us
    psum x1 -> x2, blocking collectives: 354 us -> 90.3 us  [the longest x1 74.4 us: on_device(): high = lax.psum(gain_running, 'ctx')]
  transfers between devices with their start and end apart: 135 -> 135, of which waited for: 110 -> 110; matrix products, arithmetic and copies ran while one was open for 1% -> 2% of each run, Pallas kernels for 0% -> 0%
where the time goes in v1:
time: 904 us; the launch traced here: 902 us
  starting transfers between devices  263 us (29%)
  blocking collectives  260 us (29%)
  waiting for transfers between devices  180 us (20%)
  loops' own time  85 us (9%)
  other arithmetic  51.5 us (6%)
  matrix products  46.7 us (5%)
  local copies, waits for them, and re-layouts  10.6 us (1%)
    ppermute x128, starting transfers between devices, passed_along(): lax.ppermute(value, axis, [(i, (i + by) % count) for i in range(count)])  236 us
    ppermute x128, waiting for transfers between devices, passed_along(): lax.ppermute(value, axis, [(i, (i + by) % count) for i in range(count)])  159 us
    all_gather x2, blocking collectives, segment_tick(): lax.all_gather(key_local, 'ctx', axis=0, tiled=True)  87.6 us
    all_gather x2, blocking collectives, segment_tick(): lax.all_gather(value_local, 'ctx', axis=0, tiled=True)  82.4 us
    another operation x2, loops' own time, segment_tick(): lax.fori_loop(0, cycle_count, cycle_turn, (key_local, value_local, zero_k...  82.4 us
    psum x1, blocking collectives, on_device(): high = lax.psum(gain_running, 'ctx')  74.4 us
    reduce_max x33, other arithmetic, block_active(): jnp.max(key_pos) >= jnp.min(query_start)  23.7 us
  transfers between devices with their start and end apart: 135, of which 110 were waited for; matrix products, arithmetic and copies ran while one was open for 2% of the time, Pallas kernels for 0%

profile of v1, /device:TPU:8, one launch (start us, length us, event | category | flops | bytes accessed | tf_op | source)
XLA Modules:
  0.0 902.3 jit_solution(13295326929773803791)
XLA Ops:
  21.4 46.2 %all-gather = bf16[1,1,2048,128]{3,2,1,0:T(8,128)(2,1)S(1)} all-gather(bf16[1,1,128,128]{3,2,1,0:T(8,128)(2,1)S(1)} %get-tuple-element.1508), channel_id=2, replica_groups=mesh['pipe'=4,'ctx'=16,'tp'=4] {'ctx'}, dimensions={2}, use_global_device_ids=true | all-gather | bytes 557056 | tf_op jit(solution)/shard_map/all_gather | solution.py:141
  72.2 40.6 %all-gather.1 = bf16[1,1,2048,128]{3,2,1,0:T(8,128)(2,1)} all-gather(bf16[1,1,128,128]{3,2,1,0:T(8,128)(2,1)S(1)} %get-tuple-element.1495), channel_id=3, replica_groups=mesh['pipe'=4,'ctx'=16,'tp'=4] {'ctx'}, dimensions={2}, use_global_device_ids=true | all-gather | bytes 557056 | tf_op jit(solution)/shard_map/all_gather | solution.py:142
  113.0 6.8 conditional.4
  120.0 273.9 %while.50 = (s32[]{:T(128)}, bf16[128,128]{1,0:T(8,128)(2,1)S(1)}, bf16[128,128]{1,0:T(8,128)(2,1)S(1)}, f32[128,128]{1,0:T(8,128)S(1)}, f32[128,128]{1,0:T(8,12...) while((s32[]{:T(128)}, bf16[128,128]{1,0:T(8,128)(2,1)S(1)}, ...), condition=%wide.region_17.18_spmd.clone, body=%wide.region_12.17_spmd.clone.sunk | while | flops 169071120 | bytes 6050608 | solution.py:173
  211.9 4.9 collective-permute-start.3
  219.8 4.8 collective-permute-done
  249.4 4.5 collective-permute-start.1
  282.3 4.7 collective-permute-start.1
  386.3 4.7 collective-permute-start.1
  394.9 5.4 all-to-all-start.2
  400.3 6.7 all-to-all-done.2
  411.5 41.4 %all-gather.2 = bf16[1,1,2048,128]{3,2,1,0:T(8,128)(2,1)S(1)} all-gather(bf16[1,1,128,128]{3,2,1,0:T(8,128)(2,1)S(1)} %get-tuple-element.1505), channel_id=4, replica_groups=mesh['pipe'=4,'ctx'=16,'tp'=4] {'ctx'}, dimensions={2}, use_global_device_ids=true | all-gather | bytes 557056 | tf_op jit(solution)/shard_map/all_gather | solution.py:141
  454.9 41.8 %all-gather.3 = bf16[1,1,2048,128]{3,2,1,0:T(8,128)(2,1)} all-gather(bf16[1,1,128,128]{3,2,1,0:T(8,128)(2,1)S(1)} %get-tuple-element.1492), channel_id=5, replica_groups=mesh['pipe'=4,'ctx'=16,'tp'=4] {'ctx'}, dimensions={2}, use_global_device_ids=true | all-gather | bytes 557056 | tf_op jit(solution)/shard_map/all_gather | solution.py:142
  512.4 5.1 all-to-all-done.4
  518.6 6.9 conditional.5
  525.6 273.6 %while.51 = (s32[]{:T(128)}, bf16[128,128]{1,0:T(8,128)(2,1)S(1)}, bf16[128,128]{1,0:T(8,128)(2,1)S(1)}, f32[128,128]{1,0:T(8,128)S(1)}, f32[128,128]{1,0:T(8,12...) while((s32[]{:T(128)}, bf16[128,128]{1,0:T(8,128)(2,1)S(1)}, ...), condition=%wide.region_33.34_spmd.clone, body=%wide.region_28.33_spmd.clone.sunk | while | flops 169071120 | bytes 6050608 | solution.py:173
  550.4 4.7 collective-permute-start.5
  616.8 4.9 collective-permute-start.7
  655.0 4.7 collective-permute-start.5
  753.7 4.9 collective-permute-start.7
  791.7 4.8 collective-permute-start.5
  805.0 5.3 all-to-all-done.5
  810.8 74.4 %psum.14 = f32[4096]{0:T(1024)S(1)} all-reduce(f32[4096]{0:T(1024)S(1)} %bitcast.428), channel_id=1, replica_groups=mesh['pipe'=4,'ctx'=16,'tp'=4] {'ctx'}, use_global_device_ids=true, to_apply=%region_37.38 | all-reduce | flops 4096 | bytes 32768 | tf_op jit(solution)/shard_map/psum | solution.py:216
  885.2 15.9 %psum.15 = f32[1,4096]{1,0:T(1,128)} all-reduce(f32[1,4096]{1,0:T(1,128)S(1)} %bitcast.429), channel_id=1, replica_groups=mesh['pipe'=4,'ctx'=16,'tp'=4] {'tp'}, use_global_device_ids=true, to_apply=%region_38.39 | all-reduce | flops 4096 | bytes 32768 | tf_op jit(solution)/shard_map/psum | solution.py:217
  (997 shorter events, 526.5 us)
Async XLA Ops:
  6.3 61.3 %all-to-all-start = ((bf16[32,4,1024]{2,0,1:T(8,128)(2,1)}), bf16[32,4,1024]{2,0,1:T(8,128)(2,1)S(1)}, u32[]{:S(2)}, u32[]{:S(2)}) async-start(bf16[32,4,1024]{2,0,1:T(8,128)(2,1)} %multiply_convert_fusion.1), calls=%async_computation | async-start | bytes 524288 | tf_op jit(solution)/shard_map/all_to_all | solution.py:123
  67.7 45.2 %all-to-all-start.1 = ((bf16[32,4,1024]{2,0,1:T(8,128)(2,1)}), bf16[32,4,1024]{2,0,1:T(8,128)(2,1)S(1)}, u32[]{:S(2)}, u32[]{:S(2)}) async-start(bf16[32,4,1024]{2,0,1:T(8,128)(2,1)} %copy.84), calls=%async_computation.1 | async-start | bytes 524288 | tf_op jit(solution)/shard_map/all_to_all | solution.py:124
  143.1 9.3 %collective-permute-start.3 = (f32[128,128]{1,0:T(8,128)S(1)}, f32[128,128]{1,0:T(8,128)S(1)}, u32[]{:S(2)}, u32[]{:S(2)}) collective-permute-start(f32[128,128]{1,0:T(8,128)S(1)} %get-tuple-element.1701), channel_id=1, source_target_pairs={{0,4},{4,8},{8,12},{12,16},{16,20},{20,24},{24,28},{28,32},{32,36}... | collective-permute-start | bytes 196616 | tf_op jit(solution)/shard_map/while/body/eval_jaxpr/ppermute | solution.py:15
  157.8 9.0 collective-permute-start.2
  192.7 8.8 collective-permute-start.2
  245.0 9.0 collective-permute-start.2
  245.1 8.9 collective-permute-start.3
  279.8 9.8 %collective-permute-start.3 = (f32[128,128]{1,0:T(8,128)S(1)}, f32[128,128]{1,0:T(8,128)S(1)}, u32[]{:S(2)}, u32[]{:S(2)}) collective-permute-start(f32[128,128]{1,0:T(8,128)S(1)} %get-tuple-element.1701), channel_id=1, source_target_pairs={{0,4},{4,8},{8,12},{12,16},{16,20},{20,24},{24,28},{28,32},{32,36}... | collective-permute-start | bytes 196616 | tf_op jit(solution)/shard_map/while/body/eval_jaxpr/ppermute | solution.py:15
  295.0 10.4 %collective-permute-start.2 = (f32[128,128]{1,0:T(8,128)S(1)}, f32[128,128]{1,0:T(8,128)S(1)}, u32[]{:S(2)}, u32[]{:S(2)}) collective-permute-start(f32[128,128]{1,0:T(8,128)S(1)} %get-tuple-element.1700), channel_id=1, source_target_pairs={{0,4},{4,8},{8,12},{12,16},{16,20},{20,24},{24,28},{28,32},{32,36}... | collective-permute-start | bytes 196616 | tf_op jit(solution)/shard_map/while/body/eval_jaxpr/ppermute | solution.py:15
  346.5 9.0 collective-permute-start.2
  380.8 10.3 %collective-permute-start.2 = (f32[128,128]{1,0:T(8,128)S(1)}, f32[128,128]{1,0:T(8,128)S(1)}, u32[]{:S(2)}, u32[]{:S(2)}) collective-permute-start(f32[128,128]{1,0:T(8,128)S(1)} %get-tuple-element.1700), channel_id=1, source_target_pairs={{0,4},{4,8},{8,12},{12,16},{16,20},{20,24},{24,28},{28,32},{32,36}... | collective-permute-start | bytes 196616 | tf_op jit(solution)/shard_map/while/body/eval_jaxpr/ppermute | solution.py:15
  381.0 10.1 %collective-permute-start.3 = (f32[128,128]{1,0:T(8,128)S(1)}, f32[128,128]{1,0:T(8,128)S(1)}, u32[]{:S(2)}, u32[]{:S(2)}) collective-permute-start(f32[128,128]{1,0:T(8,128)S(1)} %get-tuple-element.1701), channel_id=1, source_target_pairs={{0,4},{4,8},{8,12},{12,16},{16,20},{20,24},{24,28},{28,32},{32,36}... | collective-permute-start | bytes 196616 | tf_op jit(solution)/shard_map/while/body/eval_jaxpr/ppermute | solution.py:15
  394.9 12.0 %all-to-all-start.2 = ((bf16[4,32,1024]{2,1,0:T(8,128)(2,1)}), bf16[4,32,1024]{2,1,0:T(8,128)(2,1)S(1)}, u32[]{:S(2)}, u32[]{:S(2)}) async-start(bf16[4,32,1024]{2,1,0:T(8,128)(2,1)} %convert_element_type.172), calls=%async_computation.2 | async-start | bytes 524288 | tf_op jit(solution)/shard_map/all_to_all | solution.py:178
  409.6 91.3 %collective-permute-start.8 = (bf16[32,4096]{1,0:T(8,128)(2,1)}, bf16[32,4096]{1,0:T(8,128)(2,1)}, u32[]{:S(2)}, u32[]{:S(2)}) collective-permute-start(bf16[32,4096]{1,0:T(8,128)(2,1)} %fusion.122), channel_id=1, source_target_pairs={{64,0},{128,64},{192,128},{65,1},{129,65},{193,129},{66,2},{130,66... | collective-permute-start | bytes 786440 | tf_op jit(solution)/shard_map/ppermute | solution.py:21
  496.7 10.1 %all-to-all-start.3 = ((bf16[32,4,1024]{2,0,1:T(8,128)(2,1)}), bf16[32,4,1024]{2,0,1:T(8,128)(2,1)S(1)}, u32[]{:S(2)}, u32[]{:S(2)}) async-start(bf16[32,4,1024]{2,0,1:T(8,128)(2,1)} %get-tuple-element.1500), calls=%async_computation.3 | async-start | bytes 524288 | tf_op jit(solution)/shard_map/all_to_all | solution.py:123
  506.8 10.8 %all-to-all-start.4 = ((bf16[32,4,1024]{2,0,1:T(8,128)(2,1)}), bf16[32,4,1024]{2,0,1:T(8,128)(2,1)}, u32[]{:S(2)}, u32[]{:S(2)}) async-start(bf16[32,4,1024]{2,0,1:T(8,128)(2,1)} %bitcast.397), calls=%async_computation.4 | async-start | bytes 524288 | tf_op jit(solution)/shard_map/all_to_all | solution.py:124
  562.7 9.6 %collective-permute-start.6 = (f32[128,128]{1,0:T(8,128)S(1)}, f32[128,128]{1,0:T(8,128)S(1)}, u32[]{:S(2)}, u32[]{:S(2)}) collective-permute-start(f32[128,128]{1,0:T(8,128)S(1)} %get-tuple-element.1724), channel_id=1, source_target_pairs={{0,4},{4,8},{8,12},{12,16},{16,20},{20,24},{24,28},{28,32},{32,36}... | collective-permute-start | bytes 196616 | tf_op jit(solution)/shard_map/while/body/eval_jaxpr/ppermute | solution.py:15
  649.9 9.8 %collective-permute-start.6 = (f32[128,128]{1,0:T(8,128)S(1)}, f32[128,128]{1,0:T(8,128)S(1)}, u32[]{:S(2)}, u32[]{:S(2)}) collective-permute-start(f32[128,128]{1,0:T(8,128)S(1)} %get-tuple-element.1724), channel_id=1, source_target_pairs={{0,4},{4,8},{8,12},{12,16},{16,20},{20,24},{24,28},{28,32},{32,36}... | collective-permute-start | bytes 196616 | tf_op jit(solution)/shard_map/while/body/eval_jaxpr/ppermute | solution.py:15
  650.0 9.8 %collective-permute-start.7 = (f32[128,128]{1,0:T(8,128)S(1)}, f32[128,128]{1,0:T(8,128)S(1)}, u32[]{:S(2)}, u32[]{:S(2)}) collective-permute-start(f32[128,128]{1,0:T(8,128)S(1)} %get-tuple-element.1725), channel_id=1, source_target_pairs={{0,4},{4,8},{8,12},{12,16},{16,20},{20,24},{24,28},{28,32},{32,36}... | collective-permute-start | bytes 196616 | tf_op jit(solution)/shard_map/while/body/eval_jaxpr/ppermute | solution.py:15
  685.4 8.9 collective-permute-start.7
  700.6 9.8 %collective-permute-start.6 = (f32[128,128]{1,0:T(8,128)S(1)}, f32[128,128]{1,0:T(8,128)S(1)}, u32[]{:S(2)}, u32[]{:S(2)}) collective-permute-start(f32[128,128]{1,0:T(8,128)S(1)} %get-tuple-element.1724), channel_id=1, source_target_pairs={{0,4},{4,8},{8,12},{12,16},{16,20},{20,24},{24,28},{28,32},{32,36}... | collective-permute-start | bytes 196616 | tf_op jit(solution)/shard_map/while/body/eval_jaxpr/ppermute | solution.py:15
  786.7 9.7 %collective-permute-start.6 = (f32[128,128]{1,0:T(8,128)S(1)}, f32[128,128]{1,0:T(8,128)S(1)}, u32[]{:S(2)}, u32[]{:S(2)}) collective-permute-start(f32[128,128]{1,0:T(8,128)S(1)} %get-tuple-element.1724), channel_id=1, source_target_pairs={{0,4},{4,8},{8,12},{12,16},{16,20},{20,24},{24,28},{28,32},{32,36}... | collective-permute-start | bytes 196616 | tf_op jit(solution)/shard_map/while/body/eval_jaxpr/ppermute | solution.py:15
  786.8 9.6 %collective-permute-start.7 = (f32[128,128]{1,0:T(8,128)S(1)}, f32[128,128]{1,0:T(8,128)S(1)}, u32[]{:S(2)}, u32[]{:S(2)}) collective-permute-start(f32[128,128]{1,0:T(8,128)S(1)} %get-tuple-element.1725), channel_id=1, source_target_pairs={{0,4},{4,8},{8,12},{12,16},{16,20},{20,24},{24,28},{28,32},{32,36}... | collective-permute-start | bytes 196616 | tf_op jit(solution)/shard_map/while/body/eval_jaxpr/ppermute | solution.py:15
  800.3 10.1 %all-to-all-start.5 = ((bf16[4,32,1024]{2,1,0:T(8,128)(2,1)}), bf16[4,32,1024]{2,1,0:T(8,128)(2,1)S(1)}, u32[]{:S(2)}, u32[]{:S(2)}) async-start(bf16[4,32,1024]{2,1,0:T(8,128)(2,1)} %convert_element_type.193), calls=%async_computation.5 | async-start | bytes 524288 | tf_op jit(solution)/shard_map/all_to_all | solution.py:178
  (122 other events, 3715.8 us)
